TPU v7x, 32 devices: a whole 2x2x4 slice. The times are simulated.
32 devices in a mesh: occ: 4 (over z), vir: 8 (over y, x, core).
Axes of the slice: x: 2, y: 2, z: 4, core: 2. Of those that a mesh axis runs over, the one named last changes fastest.
Arguments:
- amplitudes: bfloat16 [40, 40, 400, 400], P('occ', None, 'vir'), may hold values from -6 to 6
- integrals: bfloat16 [400, 400, 3200], P('vir', 'occ'), may hold values from -0.109375 to 0.109375
- batch_index: int32 [1], replicated, may hold values from 0 to 49
- eps_occ: float32 [40], replicated, may hold values from -1 to -0.3
- eps_vir: float32 [400], replicated, may hold values from 0.2 to 1.5
Outputs:
- update: float32 [400, 400, 1600], P(None, 'vir', 'occ')
Inputs may be any that keep to these rules, and one draw needn't show every extreme that they name: Selects the virtual orbitals d from 8 * batch_index to 8 * batch_index + 7.
All inputs are finite; a program needn't handle non-finite values.
Results may differ from a plain program's by a relative error of at most 0.0029.
Values may be sent and summed in bfloat16 or wider, within the bound.
A program may use at most 384 MiB of HBM per device.

v0:
```python
import jax
import jax.numpy as jnp
from jax import lax
from jax.sharding import PartitionSpec as P

NB = 8


def shards(amplitudes, integrals, batch_index, eps_occ, eps_vir):
    occ_rows = amplitudes.shape[0]
    occ_all = amplitudes.shape[1]
    vir_local = amplitudes.shape[2]
    block_a = integrals.shape[0]
    block_b = integrals.shape[1]
    begin = batch_index[0] * NB
    sliced = lax.dynamic_slice_in_dim(amplitudes, begin, NB, 3)
    sliced = sliced.reshape(occ_rows, occ_all, vir_local * NB)
    weights_flat = integrals.reshape(block_a * block_b, integrals.shape[2])
    dims_last = (((1,), (1,)), ((), ()))
    columns = lax.all_gather(sliced, "vir", axis=2, tiled=True)
    columns = columns.reshape(occ_rows * occ_all, columns.shape[2])
    ladder = lax.dot_general(
        weights_flat,
        lax.all_gather(columns, "occ", axis=0, tiled=True),
        dims_last,
        preferred_element_type=jnp.float32,
    )
    ladder = 0.5 * ladder.reshape(block_a, block_b, occ_all, occ_all)
    mixed = (ladder - jnp.transpose(ladder, (0, 1, 3, 2))).astype(jnp.bfloat16)
    mixed = mixed.reshape(block_a, block_b, occ_all * occ_all)
    own_rows = lax.all_to_all(mixed, "occ", split_axis=2, concat_axis=1, tiled=True)
    relaid = lax.all_to_all(own_rows, "vir", split_axis=1, concat_axis=0, tiled=True)
    mirrored = jnp.swapaxes(own_rows, 0, 1)
    pair_count = relaid.shape[2]
    pair_rows = pair_count // occ_all
    width_b = relaid.shape[1]
    occ_index = lax.axis_index("occ")
    vir_index = lax.axis_index("vir")
    energy_rows = lax.dynamic_slice_in_dim(eps_occ, occ_index * pair_rows, pair_rows, 0)
    pair_energy = (energy_rows[:, None] + eps_occ[None, :]).reshape(pair_count)
    energy_cols = lax.dynamic_slice_in_dim(eps_vir, vir_index * width_b, width_b, 0)
    denominator = pair_energy[None, None, :] - eps_vir[:, None, None] - energy_cols[None, :, None]
    return (relaid.astype(jnp.float32) - mirrored.astype(jnp.float32)) / denominator


def solution(mesh):
    in_specs = (P("occ", None, "vir", None), P("vir", "occ", None), P(), P(), P())
    out_specs = P(None, "vir", "occ")
    return jax.shard_map(shards, mesh=mesh, in_specs=in_specs, out_specs=out_specs, check_vma=False)
```

profile of v0, /device:TPU:0, one launch (start us, length us, event | category | flops | bytes accessed | tf_op | source)
XLA Modules:
  0.0 1484.9 jit_solution(17963957135518208131)
XLA Ops:
  6.5 0.0 all-gather.3.cloned.1.call-start
  7.2 6.2 constant_dynamic-slice_fusion
  13.4 4.9 copy.27
  18.3 0.0 all-gather.3.cloned.1.call-update
  18.3 0.0 all-gather.5.cloned.1.call-start
  18.4 56.2 %all-gather.3.cloned.1.call-done = bf16[10,40,3200]{1,2,0:T(8,128)(2,1)} async-done(((bf16[10,40,400]{1,2,0:T(8,128)(2,1)}), bf16[10,40,3200]{1,2,0:T(8,128)(2,1)}) %all-gather.3.cloned.1.call-update) | async-done | bytes 2560016 | tf_op jit(solution)/shard_map/all_gather | solution.py:20
  74.6 8.3 copy.28
  82.9 0.0 all-gather.5.cloned.1.call-update
  82.9 33.5 %reshape.69 = bf16[5000,3200]{1,0:T(8,128)(2,1)} reshape(bf16[50,100,3200]{2,1,0:T(8,128)(2,1)} %param.6) | data formatting | bytes 64000000 | tf_op jit(solution)/shard_map/reshape | solution.py:18
  116.4 146.5 %all-gather.5.cloned.1.call-done = bf16[1600,3200]{1,0:T(8,128)(2,1)} async-done(((bf16[400,3200]{1,0:T(8,128)(2,1)}), bf16[1600,3200]{1,0:T(8,128)(2,1)}) %all-gather.5.cloned.1.call-update) | async-done | bytes 10240016 | tf_op jit(solution)/shard_map/all_gather | solution.py:24
  263.0 65.0 %multiply_bitcast_fusion = f32[5000,1600]{0,1:T(8,128)} fusion(bf16[1600,3200]{1,0:T(8,128)(2,1)} %all-gather.5.cloned.1.call-done, bf16[5000,3200]{1,0:T(8,128)(2,1)} %reshape.69), kind=kOutput, calls=%fused_computation.4 | convolution fusion | flops 51207999488 | bytes 74240000 | tf_op jit(solution)/shard_map/dot_general | solution.py:22
  327.9 43.7 %mul.29 = f32[50,100,40,40]{1,0,3,2:T(8,128)} reshape(f32[5000,1600]{0,1:T(8,128)} %multiply_bitcast_fusion) | data formatting | bytes 64000000 | tf_op jit(solution)/shard_map/mul | solution.py:28
  371.7 36.6 %fusion = bf16[50,100,40,40]{1,0,3,2:T(8,128)(2,1)} fusion(f32[50,100,40,40]{1,0,3,2:T(8,128)} %mul.29), kind=kLoop, calls=%fused_computation.1 | loop fusion | flops 16000000 | bytes 48000000 | tf_op jit(solution)/shard_map/convert_element_type | solution.py:29
  408.3 509.0 %all_to_all.27 = bf16[50,100,1600]{1,0,2:T(8,128)(2,1)} all-to-all(bf16[50,100,1600]{1,0,2:T(8,128)(2,1)} %bitcast.24), channel_id=1, replica_groups=mesh['occ'=4,'vir'=8] {'occ'}, dimensions={2} | all-to-all | bytes 32000000 | tf_op jit(solution)/shard_map/all_to_all | solution.py:31
  917.3 35.0 %copy.35 = bf16[50,100,4,400]{3,2,1,0:T(4,128)(2,1)} copy(bf16[50,100,4,400]{1,0,3,2:T(8,128)(2,1)} %bitcast.25) | data formatting | bytes 32000000 | tf_op jit(solution)/shard_map/all_to_all | solution.py:31
  952.3 20.3 %copy.31 = bf16[50,4,100,400]{3,2,1,0:T(8,128)(2,1)} copy(bf16[50,4,100,400]{3,1,2,0:T(4,128)(2,1)} %bitcast.26) | data formatting | bytes 32000000 | tf_op jit(solution)/shard_map/all_to_all | solution.py:31
  972.6 28.9 %all_to_all.23 = bf16[50,400,400]{2,1,0:T(8,128)(2,1)} reshape(bf16[50,4,100,400]{3,2,1,0:T(8,128)(2,1)} %copy.31) | data formatting | bytes 32000000 | tf_op jit(solution)/shard_map/all_to_all | solution.py:31
  1001.5 30.0 %copy.32 = bf16[50,400,400]{2,0,1:T(8,128)(2,1)} copy(bf16[50,400,400]{2,1,0:T(8,128)(2,1)} %all_to_all.23) | data formatting | bytes 32000000 | tf_op jit(solution)/shard_map/all_to_all | solution.py:31
  1031.4 6.4 all-to-all-start.1
  1037.8 0.0 copy-done.1
  1037.8 0.1 dynamic_slice.10
  1037.9 0.1 broadcast_add_fusion
  1038.0 0.1 add.34
  1038.1 0.0 copy-done
  1038.1 0.1 dynamic_slice.11
  1038.2 0.1 broadcast_subtract_fusion
  1038.3 249.5 %all-to-all-done.1 = bf16[50,400,400]{2,0,1:T(8,128)(2,1)} async-done(((bf16[50,400,400]{2,0,1:T(8,128)(2,1)}), bf16[50,400,400]{2,0,1:T(8,128)(2,1)}, u32[]{:S(2)}, u32[]{:S(2)}) %all-to-all-start.1) | async-done | bytes 16000032 | tf_op jit(solution)/shard_map/all_to_all | solution.py:32
  1287.8 24.7 %copy_convert_fusion = f32[50,400,400]{2,1,0:T(8,128)} fusion(bf16[50,400,400]{2,0,1:T(8,128)(2,1)} %all-to-all-done.1), kind=kLoop, calls=%fused_computation.5 | loop fusion | flops 8000000 | bytes 48000000 | tf_op jit(solution)/shard_map/convert_element_type | solution.py:43
  1312.4 41.8 %reshape.72 = f32[50,8,50,400]{3,2,1,0:T(8,128)} reshape(f32[50,400,400]{2,1,0:T(8,128)} %copy_convert_fusion) | data formatting | bytes 64000000 | tf_op jit(solution)/shard_map/convert_element_type | solution.py:43
  1354.2 48.8 %copy.34 = f32[8,50,50,400]{3,1,0,2:T(8,128)} copy(f32[8,50,50,400]{3,2,0,1:T(8,128)} %bitcast.23) | data formatting | bytes 64000000 | tf_op jit(solution)/shard_map/convert_element_type | solution.py:43
  1403.0 41.8 %reshape.71 = f32[400,50,400]{2,0,1:T(8,128)} reshape(f32[8,50,50,400]{3,1,0,2:T(8,128)} %copy.34) | data formatting | bytes 64000000 | tf_op jit(solution)/shard_map/convert_element_type | solution.py:43
  1444.8 33.2 %fusion.1 = f32[400,50,400]{2,0,1:T(8,128)} fusion(f32[400,50,400]{2,0,1:T(8,128)} %reshape.71, bf16[50,400,400]{2,1,0:T(8,128)(2,1)} %all_to_all.23, f32[50]{0:T(128)S(1)} %dynamic_slice.11, f32[400,400]{1,0:T(8,128)S(1)} %broadcast_subtract_fusion), kind=kLoop, calls=%fused_computation.3 | loop fusion | flops 32000000 | bytes 80640200 | tf_op jit(solution)/shard_map/div | solution.py:43
  (2 shorter events, 0.0 us)
Async XLA Ops:
  6.5 68.1 %all-gather.3.cloned.1.call-start = ((), (), s32[]{:S(2)}) async-start(), calls=%async_computation.2 | async-start | bytes 9216000 | tf_op jit(solution)/shard_map/all_gather | solution.py:20
  18.3 244.6 %all-gather.5.cloned.1.call-start = ((), (), s32[]{:S(2)}) async-start(), calls=%async_computation.3 | async-start | bytes 12800000 | tf_op jit(solution)/shard_map/all_gather | solution.py:24
  1031.4 6.4 copy-start.1
  1031.4 6.6 copy-start
  1031.4 256.3 %all-to-all-start.1 = ((bf16[50,400,400]{2,0,1:T(8,128)(2,1)}), bf16[50,400,400]{2,0,1:T(8,128)(2,1)}, u32[]{:S(2)}, u32[]{:S(2)}) async-start(bf16[50,400,400]{2,0,1:T(8,128)(2,1)} %copy.32), calls=%async_computation.1 | async-start | bytes 45875200 | tf_op jit(solution)/shard_map/all_to_all | solution.py:32
Sparse Core Ops, SparseCore 0:
  18.5 56.1 all-gather.2
  83.1 179.8 all-gather.4
where the time goes:
time: 1490 us; the launch traced here: 1480 us
  blocking collectives  509 us (34%)
  waiting for transfers between devices  452 us (30%)
  local copies, waits for them, and re-layouts  343 us (23%)
  other arithmetic  94.7 us (6%)
  matrix products  65 us (4%)
    all_to_all x1, blocking collectives, shards(): lax.all_to_all(mixed, 'occ', split_axis=2, concat_axis=1, tiled=True)  509 us
    all_to_all x1, waiting for transfers between devices, shards(): lax.all_to_all(own_rows, 'vir', split_axis=1, concat_axis=0, tiled=True)  249 us
    all_gather x1, waiting for transfers between devices, shards(): lax.all_gather(columns, 'occ', axis=0, tiled=True)  147 us
    convert_element_type x3, local copies, waits for them, and re-layouts, shards(): relaid.astype(jnp.float32) - mirrored.astype(jnp.float32)  132 us
    all_to_all x4, local copies, waits for them, and re-layouts, shards(): lax.all_to_all(mixed, 'occ', split_axis=2, concat_axis=1, tiled=True)  114 us
    dot_general x1, matrix products, shards(): lax.dot_general(weights_flat, lax.all_gather(columns, 'occ', axis=0, tile...  65 us
    all_gather x1, waiting for transfers between devices, shards(): columns = lax.all_gather(sliced, 'vir', axis=2, tiled=True)  56.2 us
    mul x1, local copies, waits for them, and re-layouts, shards(): ladder = 0.5 * ladder.reshape(block_a, block_b, occ_all, occ_all)  43.7 us
  transfers between devices with their start and end apart: 3, of which 3 were waited for; matrix products, arithmetic and copies ran while one was open for 2% of the time, Pallas kernels for 0%

commit v1 on v0

--- a/solution.py
+++ b/solution.py
@@ -28,7 +28,19 @@
     ladder = 0.5 * ladder.reshape(block_a, block_b, occ_all, occ_all)
     mixed = (ladder - jnp.transpose(ladder, (0, 1, 3, 2))).astype(jnp.bfloat16)
     mixed = mixed.reshape(block_a, block_b, occ_all * occ_all)
-    own_rows = lax.all_to_all(mixed, "occ", split_axis=2, concat_axis=1, tiled=True)
+    ways, here = (lax.axis_size("occ"), lax.axis_index("occ"))
+    width = mixed.shape[2] // ways
+    dims = list(mixed.shape)
+    dims[2] = width
+    height = dims[1]
+    dims[1] = height * ways
+    full = jnp.zeros(dims, mixed.dtype)
+    for mask in range(ways):
+        part = lax.dynamic_slice_in_dim(mixed, (here ^ mask) * width, width, axis=2)
+        if mask:
+            part = lax.ppermute(part, "occ", [(d, d ^ mask) for d in range(ways)])
+        full = lax.dynamic_update_slice_in_dim(full, part, (here ^ mask) * height, axis=1)
+    own_rows = full
     relaid = lax.all_to_all(own_rows, "vir", split_axis=1, concat_axis=0, tiled=True)
     mirrored = jnp.swapaxes(own_rows, 0, 1)
     pair_count = relaid.shape[2]

time: 1490 us -> 1400 us (0.940)
  the two profiles are of different devices: /device:TPU:0 before, /device:TPU:8 now
where the time goes in v1:
time: 1400 us; the launch traced here: 1390 us
  waiting for transfers between devices  753 us (54%)
  local copies, waits for them, and re-layouts  456 us (33%)
  other arithmetic  94.7 us (7%)
  matrix products  65 us (5%)
  between operations  14.1 us (1%)
    ppermute x3, waiting for transfers between devices, shards(): part = lax.ppermute(part, 'occ', [(d, d ^ mask) for d in range(ways)])  305 us
    all_to_all x1, waiting for transfers between devices, shards(): lax.all_to_all(own_rows, 'vir', split_axis=1, concat_axis=0, tiled=True)  249 us
    dynamic_update_slice x5, local copies, waits for them, and re-layouts, shards(): lax.dynamic_update_slice_in_dim(full, part, (here ^ mask) * height, axis=1)  168 us
    all_gather x1, waiting for transfers between devices, shards(): lax.all_gather(columns, 'occ', axis=0, tiled=True)  144 us
    convert_element_type x3, local copies, waits for them, and re-layouts, shards(): relaid.astype(jnp.float32) - mirrored.astype(jnp.float32)  132 us
    dot_general x1, matrix products, shards(): lax.dot_general(weights_flat, lax.all_gather(columns, 'occ', axis=0, tile...  65 us
    all_gather x1, waiting for transfers between devices, shards(): columns = lax.all_gather(sliced, 'vir', axis=2, tiled=True)  54.7 us
    mul x1, local copies, waits for them, and re-layouts, shards(): ladder = 0.5 * ladder.reshape(block_a, block_b, occ_all, occ_all)  43.7 us
  transfers between devices with their start and end apart: 6, of which 6 were waited for; matrix products, arithmetic and copies ran while one was open for 12% of the time, Pallas kernels for 0%

profile of v1, /device:TPU:8, one launch (start us, length us, event | category | flops | bytes accessed | tf_op | source)
XLA Modules:
  0.0 1394.7 jit_solution(598452933471791661)
XLA Ops:
  7.2 6.2 constant_dynamic-slice_fusion.4
  13.4 5.0 copy.37
  18.4 54.7 %all-gather.3.cloned.1.call-done = bf16[10,40,3200]{1,2,0:T(8,128)(2,1)} async-done(((bf16[10,40,400]{1,2,0:T(8,128)(2,1)}), bf16[10,40,3200]{1,2,0:T(8,128)(2,1)}) %all-gather.3.cloned.1.call-update) | async-done | bytes 2560016 | tf_op jit(solution)/shard_map/all_gather | solution.py:20
  73.1 8.3 copy.38
  81.4 33.5 %reshape.69 = bf16[5000,3200]{1,0:T(8,128)(2,1)} reshape(bf16[50,100,3200]{2,1,0:T(8,128)(2,1)} %param.6) | data formatting | bytes 64000000 | tf_op jit(solution)/shard_map/reshape | solution.py:18
  114.9 143.6 %all-gather.5.cloned.1.call-done = bf16[1600,3200]{1,0:T(8,128)(2,1)} async-done(((bf16[400,3200]{1,0:T(8,128)(2,1)}), bf16[1600,3200]{1,0:T(8,128)(2,1)}) %all-gather.5.cloned.1.call-update) | async-done | bytes 10240016 | tf_op jit(solution)/shard_map/all_gather | solution.py:24
  258.5 65.0 %multiply_bitcast_fusion = f32[5000,1600]{0,1:T(8,128)} fusion(bf16[1600,3200]{1,0:T(8,128)(2,1)} %all-gather.5.cloned.1.call-done, bf16[5000,3200]{1,0:T(8,128)(2,1)} %reshape.69), kind=kOutput, calls=%fused_computation.4 | convolution fusion | flops 51207999488 | bytes 74240000 | tf_op jit(solution)/shard_map/dot_general | solution.py:22
  323.4 43.7 %mul.53 = f32[50,100,40,40]{1,0,3,2:T(8,128)} reshape(f32[5000,1600]{0,1:T(8,128)} %multiply_bitcast_fusion) | data formatting | bytes 64000000 | tf_op jit(solution)/shard_map/mul | solution.py:28
  367.1 36.6 %fusion = bf16[50,100,40,40]{1,0,3,2:T(8,128)(2,1)} fusion(f32[50,100,40,40]{1,0,3,2:T(8,128)} %mul.53), kind=kLoop, calls=%fused_computation.1 | loop fusion | flops 16000000 | bytes 48000000 | tf_op jit(solution)/shard_map/convert_element_type | solution.py:29
  403.8 12.3 copy.40
  416.1 7.5 constant_dynamic-slice_fusion
  423.6 3.5 collective-permute-start
  428.6 8.1 copy.41
  436.7 7.1 broadcast_in_dim.2
  443.8 34.7 %dynamic_update_slice.12 = bf16[50,400,400]{2,1,0:T(8,128)(2,1)} dynamic-update-slice(bf16[50,400,400]{2,1,0:T(8,128)(2,1)} %broadcast_in_dim.2, bf16[50,100,400]{2,1,0:T(8,128)(2,1)} %copy.41, s32[]{:T(128)} %constant.4.clone.1, s32[]{:T(128)S(6)} %select_n.35, s32[]{:T(128)} %constant.4.clone.1) | dynamic-update-slice | bytes 8000004 | tf_op jit(solution)/shard_map/dynamic_update_slice | solution.py:42
  478.5 167.5 %collective-permute-done = bf16[50,100,400]{1,2,0:T(8,128)(2,1)} collective-permute-done((bf16[50,100,400]{1,2,0:T(8,128)(2,1)}, bf16[50,100,400]{1,2,0:T(8,128)(2,1)}, u32[]{:S(2)}, u32[]{:S(2)}) %collective-permute-start) | collective-permute-done | bytes 4000032 | tf_op jit(solution)/shard_map/ppermute | solution.py:41
  646.0 8.1 copy.42
  654.2 34.7 %dynamic_update_slice.13 = bf16[50,400,400]{2,1,0:T(8,128)(2,1)} dynamic-update-slice(bf16[50,400,400]{2,1,0:T(8,128)(2,1)} %dynamic_update_slice.12, bf16[50,100,400]{2,1,0:T(8,128)(2,1)} %copy.42, s32[]{:T(128)} %constant.4.clone.1, s32[]{:T(128)S(6)} %select_n.37, s32[]{:T(128)} %constant.4.clone.1) | dynamic-update-slice | bytes 8000004 | tf_op jit(solution)/shard_map/dynamic_update_slice | solution.py:42
  688.9 69.4 %collective-permute-done.1 = bf16[50,100,400]{1,2,0:T(8,128)(2,1)} collective-permute-done((bf16[50,100,400]{1,2,0:T(8,128)(2,1)}, bf16[50,100,400]{1,2,0:T(8,128)(2,1)}, u32[]{:S(2)}, u32[]{:S(2)}) %collective-permute-start.1) | collective-permute-done | bytes 4000032 | tf_op jit(solution)/shard_map/ppermute | solution.py:41
  758.3 8.1 copy.43
  766.4 33.5 %dynamic_update_slice.14 = bf16[50,400,400]{2,1,0:T(8,128)(2,1)} dynamic-update-slice(bf16[50,400,400]{2,1,0:T(8,128)(2,1)} %dynamic_update_slice.13, bf16[50,100,400]{2,1,0:T(8,128)(2,1)} %copy.43, s32[]{:T(128)} %constant.4.clone.1, s32[]{:T(128)S(6)} %select_n.39, s32[]{:T(128)} %constant.4.clone.1) | dynamic-update-slice | bytes 8000004 | tf_op jit(solution)/shard_map/dynamic_update_slice | solution.py:42
  799.9 68.4 %collective-permute-done.2 = bf16[50,100,400]{1,2,0:T(8,128)(2,1)} collective-permute-done((bf16[50,100,400]{1,2,0:T(8,128)(2,1)}, bf16[50,100,400]{1,2,0:T(8,128)(2,1)}, u32[]{:S(2)}, u32[]{:S(2)}) %collective-permute-start.2) | collective-permute-done | bytes 4000032 | tf_op jit(solution)/shard_map/ppermute | solution.py:41
  868.4 8.1 copy.44
  876.5 34.6 %dynamic_update_slice.15 = bf16[50,400,400]{2,1,0:T(8,128)(2,1)} dynamic-update-slice(bf16[50,400,400]{2,1,0:T(8,128)(2,1)} %dynamic_update_slice.14, bf16[50,100,400]{2,1,0:T(8,128)(2,1)} %copy.44, s32[]{:T(128)} %constant.4.clone.1, s32[]{:T(128)S(6)} %select_n.41, s32[]{:T(128)} %constant.4.clone.1) | dynamic-update-slice | bytes 8000004 | tf_op jit(solution)/shard_map/dynamic_update_slice | solution.py:42
  911.2 30.0 %copy.45 = bf16[50,400,400]{2,0,1:T(8,128)(2,1)} copy(bf16[50,400,400]{2,1,0:T(8,128)(2,1)} %dynamic_update_slice.15) | data formatting | bytes 32000000 | tf_op jit(solution)/shard_map/dynamic_update_slice | solution.py:42
  941.1 6.4 all-to-all-start
  948.0 249.5 %all-to-all-done = bf16[50,400,400]{2,0,1:T(8,128)(2,1)} async-done(((bf16[50,400,400]{2,0,1:T(8,128)(2,1)}), bf16[50,400,400]{2,0,1:T(8,128)(2,1)}, u32[]{:S(2)}, u32[]{:S(2)}) %all-to-all-start) | async-done | bytes 16000032 | tf_op jit(solution)/shard_map/all_to_all | solution.py:44
  1197.5 24.7 %copy_convert_fusion = f32[50,400,400]{2,1,0:T(8,128)} fusion(bf16[50,400,400]{2,0,1:T(8,128)(2,1)} %all-to-all-done), kind=kLoop, calls=%fused_computation.5 | loop fusion | flops 8000000 | bytes 48000000 | tf_op jit(solution)/shard_map/convert_element_type | solution.py:55
  1222.1 41.8 %reshape.72 = f32[50,8,50,400]{3,2,1,0:T(8,128)} reshape(f32[50,400,400]{2,1,0:T(8,128)} %copy_convert_fusion) | data formatting | bytes 64000000 | tf_op jit(solution)/shard_map/convert_element_type | solution.py:55
  1263.9 48.9 %copy.47 = f32[8,50,50,400]{3,1,0,2:T(8,128)} copy(f32[8,50,50,400]{3,2,0,1:T(8,128)} %bitcast.21) | data formatting | bytes 64000000 | tf_op jit(solution)/shard_map/convert_element_type | solution.py:55
  1312.8 41.8 %reshape.71 = f32[400,50,400]{2,0,1:T(8,128)} reshape(f32[8,50,50,400]{3,1,0,2:T(8,128)} %copy.47) | data formatting | bytes 64000000 | tf_op jit(solution)/shard_map/convert_element_type | solution.py:55
  1354.6 33.2 %fusion.1 = f32[400,50,400]{2,0,1:T(8,128)} fusion(f32[400,50,400]{2,0,1:T(8,128)} %reshape.71, bf16[50,400,400]{2,1,0:T(8,128)(2,1)} %dynamic_update_slice.15, f32[50]{0:T(128)S(1)} %dynamic_slice.27, f32[400,400]{1,0:T(8,128)S(1)} %broadcast_subtract_fusion), kind=kLoop, calls=%fused_computation.3 | loop fusion | flops 32000000 | bytes 80640200 | tf_op jit(solution)/shard_map/div | solution.py:55
  (15 shorter events, 2.0 us)
Async XLA Ops:
  6.5 66.6 %all-gather.3.cloned.1.call-start = ((), (), s32[]{:S(2)}) async-start(), calls=%async_computation.1 | async-start | bytes 9216000 | tf_op jit(solution)/shard_map/all_gather | solution.py:20
  18.4 240.1 %all-gather.5.cloned.1.call-start = ((), (), s32[]{:S(2)}) async-start(), calls=%async_computation.2 | async-start | bytes 12800000 | tf_op jit(solution)/shard_map/all_gather | solution.py:24
  423.6 222.4 %collective-permute-start = (bf16[50,100,400]{1,2,0:T(8,128)(2,1)}, bf16[50,100,400]{1,2,0:T(8,128)(2,1)}, u32[]{:S(2)}, u32[]{:S(2)}) collective-permute-start(bf16[50,100,400]{1,2,0:T(8,128)(2,1)} %get-tuple-element.7), channel_id=1, source_target_pairs={{0,8},{8,0},{16,24},{24,16},{1,9},{9,1},{17,25},{25,17},{2,10},{10... | collective-permute-start | bytes 12000008 | tf_op jit(solution)/shard_map/ppermute | solution.py:41
  427.1 331.2 %collective-permute-start.1 = (bf16[50,100,400]{1,2,0:T(8,128)(2,1)}, bf16[50,100,400]{1,2,0:T(8,128)(2,1)}, u32[]{:S(2)}, u32[]{:S(2)}) collective-permute-start(bf16[50,100,400]{1,2,0:T(8,128)(2,1)} %get-tuple-element.6), channel_id=1, source_target_pairs={{0,16},{8,24},{16,0},{24,8},{1,17},{9,25},{17,1},{25,9},{2,18},{10... | collective-permute-start | bytes 12000008 | tf_op jit(solution)/shard_map/ppermute | solution.py:41
  427.7 440.7 %collective-permute-start.2 = (bf16[50,100,400]{1,2,0:T(8,128)(2,1)}, bf16[50,100,400]{1,2,0:T(8,128)(2,1)}, u32[]{:S(2)}, u32[]{:S(2)}) collective-permute-start(bf16[50,100,400]{1,2,0:T(8,128)(2,1)} %get-tuple-element.5), channel_id=1, source_target_pairs={{0,24},{8,16},{16,8},{24,0},{1,25},{9,17},{17,9},{25,1},{2,26},{10... | collective-permute-start | bytes 12000008 | tf_op jit(solution)/shard_map/ppermute | solution.py:41
  941.1 6.4 copy-start.1
  941.1 6.7 copy-start
  941.1 256.3 %all-to-all-start = ((bf16[50,400,400]{2,0,1:T(8,128)(2,1)}), bf16[50,400,400]{2,0,1:T(8,128)(2,1)}, u32[]{:S(2)}, u32[]{:S(2)}) async-start(bf16[50,400,400]{2,0,1:T(8,128)(2,1)} %copy.45), calls=%async_computation | async-start | bytes 45875200 | tf_op jit(solution)/shard_map/all_to_all | solution.py:44
Sparse Core Ops, SparseCore 0:
  18.5 54.5 all-gather.2
  81.5 176.9 all-gather.4
